TPU v7x, 128 devices: a whole 4x4x4 slice. The times are simulated.
128 devices in a mesh: node: 32 (over z, y_lo, x), rep: 4 (over y_hi, core).
Axes of the slice: x: 4, y: 4 (y_hi: 2, y_lo: 2; y = y_hi * 2 + y_lo), z: 4, core: 2. Of those that a mesh axis runs over, the one named last changes fastest.
Arguments:
- node_feats: bfloat16 [65536, 256], P('node'), may hold values from -6 to 6
- weight: bfloat16 [256, 256], replicated, may hold values from -0.375 to 0.375
- cotangent: bfloat16 [65536, 256], P(('node', 'rep')), may hold values from -6 to 6
- tiles: bfloat16 [32, 4, 160, 256, 256], P('node', 'rep'), may hold values from -0.049804688 to 0.049804688
- tile_rows: int32 [32, 4, 160], P('node', 'rep'), may hold values from 0 to 7
- tile_cols: int32 [32, 4, 160], P('node', 'rep'), may hold values from 0 to 63
- tile_count: int32 [32, 4], P('node', 'rep'), may hold values from 80 to 160, as said below
Outputs:
- activated: bfloat16 [65536, 256], P(('node', 'rep'))
- feature_grad: bfloat16 [65536, 256], P(('node', 'rep'))
- weight_grad: float32 [256, 256], replicated
Inputs may be any that keep to these rules, and one draw needn't show every extreme that they name: `tile_count`: slots at and beyond a device's count are ignored; some device has all 160 slots live in every draw.
All inputs are finite; a program needn't handle non-finite values.
Results may differ from a plain program's by a relative error of at most 0.007.
Values may be sent and summed in bfloat16 or wider, within the bound.
No kernel may reach another device: no remote copies, remote signals or barrier semaphores. Data moves between devices by JAX's collectives and lax.ppermute only.
A program may use at most 256 MiB of HBM per device.

v0:
```python
import jax
import jax.numpy as jnp
from jax import lax
from jax.sharding import PartitionSpec as P


def body(node_feats, weight, cotangent, tiles, tile_rows, tile_cols, tile_count):
    nrep = lax.axis_size("rep")
    nnode = lax.axis_size("node")
    rep_idx = lax.axis_index("rep")
    rows, feat = node_feats.shape
    block = tiles.shape[-1]
    row_blocks = rows // block
    quarter = row_blocks // nrep
    share = rows // nrep
    compact_cols = quarter * nnode
    slot_tiles = tiles[0, 0]
    slot_rows = tile_rows[0, 0]
    slot_cols = tile_cols[0, 0]
    slot_total = slot_tiles.shape[0]
    live = jnp.arange(slot_total, dtype=jnp.int32) < tile_count[0, 0]
    live_scale = live.astype(jnp.float32)[:, None, None]
    feat_blocks = node_feats.reshape(row_blocks, block, feat)
    mine = lax.dynamic_slice_in_dim(feat_blocks, rep_idx * quarter, quarter, 0)
    compact = lax.all_gather(mine, "node", axis=0, tiled=True)
    picked = compact[slot_cols]
    forward_prod = (
        jnp.einsum("tab,tbf->taf", slot_tiles, picked, preferred_element_type=jnp.float32)
        * live_scale
    )
    partial_agg = (
        jnp.zeros((row_blocks, block, feat), jnp.float32)
        .at[slot_rows]
        .add(forward_prod)
        .reshape(rows, feat)
    )
    scale = float(rows * nnode) ** (-0.5)
    aggregated = lax.psum(partial_agg, "rep").astype(jnp.bfloat16)
    cot_full = lax.all_gather(cotangent, "rep", axis=0, tiled=True)
    pre = jnp.dot(aggregated, weight, preferred_element_type=jnp.float32)
    sig = jax.nn.sigmoid(pre)
    activated_full = (pre * sig).astype(jnp.bfloat16)
    dpre = (cot_full.astype(jnp.float32) * sig * (1.0 + pre * (1.0 - sig))).astype(jnp.bfloat16)
    dagg = jnp.dot(dpre, weight.T, preferred_element_type=jnp.float32).astype(jnp.bfloat16)
    activated = lax.dynamic_slice_in_dim(activated_full, rep_idx * share, share, 0)
    agg_share = lax.dynamic_slice_in_dim(aggregated, rep_idx * share, share, 0)
    dpre_share = lax.dynamic_slice_in_dim(dpre, rep_idx * share, share, 0)
    weight_term = lax.dot_general(
        agg_share, dpre_share, (((0,), (0,)), ((), ())), preferred_element_type=jnp.float32
    )
    weight_grad = lax.psum(weight_term, ("node", "rep")) * scale
    dagg_blocks = dagg.reshape(row_blocks, block, feat)
    backward_prod = (
        jnp.einsum(
            "tab,taf->tbf", slot_tiles, dagg_blocks[slot_rows], preferred_element_type=jnp.float32
        )
        * live_scale
    )
    column_part = (
        jnp.zeros((compact_cols, block, feat), jnp.float32).at[slot_cols].add(backward_prod)
    )
    owned = lax.psum_scatter(column_part, "node", scatter_dimension=0, tiled=True)
    feature_grad = owned.reshape(quarter * block, feat).astype(jnp.bfloat16)
    return (activated, feature_grad, weight_grad)


def solution(mesh):
    placed = (
        P("node", None),
        P(),
        P(("node", "rep"), None),
        P("node", "rep", None, None, None),
        P("node", "rep", None),
        P("node", "rep", None),
        P("node", "rep"),
    )
    return jax.shard_map(
        body,
        mesh=mesh,
        in_specs=placed,
        out_specs=(P(("node", "rep"), None), P(("node", "rep"), None), P()),
        check_vma=False,
    )
```

profile of v0, /device:TPU:0, one launch (start us, length us, event | category | flops | bytes accessed | tf_op | source)
XLA Modules:
  0.0 760.6 jit_solution(5284792371590088112)
XLA Ops:
  7.2 0.0 all-gather.3.cloned.1.call-start
  7.2 1.2 copy-done
  8.4 0.7 constant_dynamic-slice_fusion
  9.1 0.0 all-gather.3.cloned.1.call-update
  9.1 0.0 all-gather.5.cloned.1.call-start
  9.2 0.7 all-gather.5.cloned.1.call-update
  9.9 0.0 all-reduce.3.cloned.1.call-start
  9.9 0.7 compare_select_fusion
  11.3 0.7 compare_select_fusion.1
  12.0 167.9 %all-gather.3.cloned.1.call-done = bf16[64,256,256]{2,1,0:T(8,128)(2,1)} async-done(((bf16[2,256,256]{2,1,0:T(8,128)(2,1)}), bf16[64,256,256]{2,1,0:T(8,128)(2,1)}) %all-gather.3.cloned.1.call-update) | async-done | bytes 8388624 | tf_op jit(solution)/shard_map/all_gather | solution.py:25
  179.9 13.0 %gather_fusion = bf16[160,256,256]{2,1,0:T(8,128)(2,1)} fusion(bf16[64,256,256]{2,1,0:T(8,128)(2,1)} %all-gather.3.cloned.1.call-done, s32[1024]{0:T(1024)S(1)} %pad_clamp_fusion.1), kind=kCustom, calls=%fused_computation | custom fusion | bytes 41943680 | tf_op jit(solution)/shard_map/gather | solution.py:26
  192.9 30.3 %multiply_bitcast_fusion.1 = f32[160,256,256]{1,2,0:T(8,128)} fusion(f32[160]{0:T(256)S(1)} %compare_convert_fusion, bf16[160,256,256]{2,1,0:T(8,128)(2,1)} %gather_fusion, bf16[1,1,160,256,256]{4,3,2,1,0:T(8,128)(2,1)} %param.10), kind=kOutput, calls=%fused_computation.5 | convolution fusion | flops 5379194880 | bytes 83886720 | tf_op jit(solution)/shard_map/tab,tbf->taf/dot_general | solution.py:28
  223.2 41.6 %copy.17 = f32[160,256,256]{2,1,0:T(8,128)} copy(f32[160,256,256]{1,2,0:T(8,128)} %multiply_bitcast_fusion.1) | data formatting | bytes 83886080 | tf_op jit(solution)/shard_map/mul | solution.py:28
  264.8 0.2 broadcast_in_dim.4
  265.0 56.7 %scatter_fusion = f32[8,256,256]{2,1,0:T(8,128)S(1)} fusion(f32[8,256,256]{2,1,0:T(8,128)S(1)} %broadcast_in_dim.4, s32[160]{0:T(256)S(1)} %bitcast.38, f32[160,256,256]{2,1,0:T(8,128)} %copy.17), kind=kCustom, calls=%fused_computation.2 | custom fusion | flops 10485760 | bytes 125829760 | tf_op jit(solution)/shard_map/scatter-add | solution.py:34
  321.7 42.3 %all-reduce.4 = bf16[2048,256]{1,0:T(8,128)(2,1)S(1)} all-reduce(f32[2048,256]{1,0:T(8,128)S(1)} %bitcast.32), channel_id=1, replica_groups=mesh['node'=32,'rep'=4] {'rep'}, use_global_device_ids=true, to_apply=%region_1.0 | all-reduce | flops 524288 | bytes 3145728 | tf_op jit(solution)/shard_map/psum | solution.py:38
  364.0 0.0 all-gather.5.cloned.1.call-done
  364.1 3.8 multiply_convert_fusion
  367.8 0.5 convolution_convert_fusion
  368.3 1.9 fusion.9
  370.2 0.0 all-reduce.3.cloned.1.call-update
  370.3 0.2 reduce-scatter.2.cloned.1.call-start
  370.5 9.6 %gather_fusion.1 = bf16[160,256,256]{2,1,0:T(8,128)(2,1)} fusion(bf16[8,256,256]{2,1,0:T(8,128)(2,1)S(1)} %bitcast.33, s32[1024]{0:T(1024)S(1)} %pad_clamp_fusion), kind=kCustom, calls=%fused_computation.1 | custom fusion | bytes 41943680 | tf_op jit(solution)/shard_map/gather | solution.py:55
  380.1 26.6 %multiply_bitcast_fusion = f32[160,256,256]{1,2,0:T(8,128)} fusion(f32[160]{0:T(256)S(1)} %compare_convert_fusion, bf16[160,256,256]{2,1,0:T(8,128)(2,1)} %gather_fusion.1, bf16[1,1,160,256,256]{4,3,2,1,0:T(8,128)(2,1)} %param.10), kind=kOutput, calls=%fused_computation.4 | convolution fusion | flops 5379194880 | bytes 83886720 | tf_op jit(solution)/shard_map/tab,taf->tbf/dot_general | solution.py:54
  406.7 41.7 %copy.19 = f32[160,256,256]{2,1,0:T(8,128)} copy(f32[160,256,256]{1,2,0:T(8,128)} %multiply_bitcast_fusion) | data formatting | bytes 83886080 | tf_op jit(solution)/shard_map/mul | solution.py:54
  448.3 7.8 %broadcast_in_dim.5 = f32[64,256,256]{2,1,0:T(8,128)} broadcast(f32[]{:T(128)} %constant.10.clone.1), dimensions={} | broadcast | bytes 16777220 | tf_op jit(solution)/shard_map/broadcast_in_dim | solution.py:60
  456.1 91.3 %scatter_fusion.1 = f32[64,256,256]{2,1,0:T(8,128)} fusion(f32[64,256,256]{2,1,0:T(8,128)} %broadcast_in_dim.5, s32[160]{0:T(256)S(1)} %bitcast.36, f32[160,256,256]{2,1,0:T(8,128)} %copy.19), kind=kCustom, calls=%fused_computation.3 | custom fusion | flops 10485760 | bytes 125829760 | tf_op jit(solution)/shard_map/scatter-add | solution.py:60
  547.4 0.0 reduce-scatter.2.cloned.1.call-update
  547.5 1.8 fusion.8
  549.3 1.7 broadcast_multiply_fusion
  550.9 201.3 %reduce-scatter.2.cloned.1.call-done = f32[2,256,256]{2,1,0:T(8,128)} async-done(((f32[64,256,256]{2,1,0:T(8,128)}), f32[2,256,256]{2,1,0:T(8,128)}) %reduce-scatter.2.cloned.1.call-update) | async-done | bytes 524304 | tf_op jit(solution)/shard_map/reduce_scatter | solution.py:62
  752.3 1.8 convert_element_type.34
  (15 shorter events, 0.0 us)
Async XLA Ops:
  7.2 1.2 copy-start
  7.2 172.7 %all-gather.3.cloned.1.call-start = ((), (), s32[]{:S(2)}) async-start(), calls=%async_computation.1 | async-start | bytes 8650752 | tf_op jit(solution)/shard_map/all_gather | solution.py:25
  9.1 354.9 %all-gather.5.cloned.1.call-start = ((), (), s32[]{:S(2)}) async-start(), calls=%async_computation.2 | async-start | bytes 1310720 | tf_op jit(solution)/shard_map/all_gather | solution.py:39
  9.9 539.4 %all-reduce.3.cloned.1.call-start = ((), (), s32[]{:S(2)}) async-start(), calls=%async_computation.4 | async-start | bytes 524288 | tf_op jit(solution)/shard_map/psum | solution.py:51
  10.6 182.3 %copy-start.4 = (s32[160,1]{0,1:T(1,128)}, s32[160,1]{0,1:T(1,128)S(1)}, u32[]{:S(2)}) copy-start(s32[160,1]{0,1:T(1,128)S(1)} %compare_select_fusion) | copy-start | bytes 1924
  265.0 99.0 %copy-start.3 = (bf16[256,256]{1,0:T(8,128)(2,1)S(1)}, bf16[256,256]{1,0:T(8,128)(2,1)}, u32[]{:S(2)}) copy-start(bf16[256,256]{1,0:T(8,128)(2,1)} %param.8) | copy-start | bytes 393220
  364.0 3.8 copy-start.2
  370.3 382.0 %reduce-scatter.2.cloned.1.call-start = ((), (), s32[]{:S(2)}) async-start(), calls=%async_computation.3 | async-start | bytes 17301504 | tf_op jit(solution)/shard_map/reduce_scatter | solution.py:62
  406.7 49.5 %copy-start.5 = (s32[160,1]{0,1:T(1,128)S(1)}, s32[160,1]{0,1:T(1,128)}, u32[]{:S(2)}) copy-start(s32[160,1]{0,1:T(1,128)} %copy-done.4) | copy-start | bytes 1924
  456.1 297.9 %copy-start.1 = (bf16[2048,256]{1,0:T(8,128)(2,1)S(1)}, bf16[2048,256]{1,0:T(8,128)(2,1)}, u32[]{:S(2)}) copy-start(bf16[2048,256]{1,0:T(8,128)(2,1)} %param.7) | copy-start | bytes 3145732
Sparse Core Ops, SparseCore 0:
  10.2 169.6 all-gather.2
  181.6 21.7 all-gather.4
  370.4 142.5 all-reduce.2
  547.6 204.6 reduce-scatter.1
where the time goes:
time: 763 us; the launch traced here: 761 us
  waiting for transfers between devices  370 us (48%)
  other arithmetic  155 us (20%)
  local copies, waits for them, and re-layouts  116 us (15%)
  matrix products  63 us (8%)
  blocking collectives  42.3 us (6%)
  between operations  14.5 us (2%)
    reduce_scatter x1, waiting for transfers between devices, body(): lax.psum_scatter(column_part, 'node', scatter_dimension=0, tiled=True)  201 us
    all_gather x1, waiting for transfers between devices, body(): compact = lax.all_gather(mine, 'node', axis=0, tiled=True)  168 us
    scatter-add x1, other arithmetic, body(): jnp.zeros((compact_cols, block, feat), jnp.float32).at[slot_cols]  91.3 us
    scatter-add x1, other arithmetic, body(): partial_agg = jnp.zeros((row_blocks, block, feat), jnp.float32).at[slot_r...  56.7 us
    psum x1, blocking collectives, body(): aggregated = lax.psum(partial_agg, 'rep').astype(jnp.bfloat16)  42.3 us
    mul x1, local copies, waits for them, and re-layouts, body(): jnp.einsum('tab,taf->tbf', slot_tiles, dagg_blocks[slot_rows], preferred_...  41.7 us
    mul x1, local copies, waits for them, and re-layouts, body(): jnp.einsum('tab,tbf->taf', slot_tiles, picked, preferred_element_type=jnp...  41.6 us
    dot_general x1, matrix products, body(): jnp.einsum('tab,tbf->taf', slot_tiles, picked, preferred_element_type=jnp...  30.3 us
  transfers between devices with their start and end apart: 4, of which 2 were waited for; matrix products, arithmetic and copies ran while one was open for 43% of the time, Pallas kernels for 0%

commit v1 on v0

--- a/solution.py
+++ b/solution.py
@@ -22,7 +22,8 @@
     live_scale = live.astype(jnp.float32)[:, None, None]
     feat_blocks = node_feats.reshape(row_blocks, block, feat)
     mine = lax.dynamic_slice_in_dim(feat_blocks, rep_idx * quarter, quarter, 0)
-    compact = lax.all_gather(mine, "node", axis=0, tiled=True)
+    repeated = jnp.stack([mine] * lax.axis_size("node"))
+    compact = jnp.concatenate(lax.all_to_all(repeated, "node", 0, 0), axis=0)
     picked = compact[slot_cols]
     forward_prod = (
         jnp.einsum("tab,tbf->taf", slot_tiles, picked, preferred_element_type=jnp.float32)

time: 763 us -> 728 us (0.954)
  waiting for transfers between devices: 370 us -> 323 us
  starting transfers between devices: 0.34 us -> 9.69 us
    all_gather x1 -> x0, waiting for transfers between devices: 168 us -> none  [body(): compact = lax.all_gather(mine, 'node', axis=0, tiled=True)]
    all_to_all x0 -> x1, waiting for transfers between devices: none -> 123 us  [body(): compact = jnp.concatenate(lax.all_to_all(repeated, 'node', 0, 0), axis=0)]
    all_to_all x0 -> x1, starting transfers between devices: none -> 9.39 us  [body(): compact = jnp.concatenate(lax.all_to_all(repeated, 'node', 0, 0), axis=0)]
  transfers between devices with their start and end apart: 4 -> 4, of which waited for: 2 -> 2; matrix products, arithmetic and copies ran while one was open for 43% -> 44% of each run, Pallas kernels for 0% -> 0%
where the time goes in v1:
time: 728 us; the launch traced here: 725 us
  waiting for transfers between devices  323 us (44%)
  other arithmetic  153 us (21%)
  local copies, waits for them, and re-layouts  119 us (16%)
  matrix products  63.1 us (9%)
  blocking collectives  42.7 us (6%)
  between operations  14.6 us (2%)
  starting transfers between devices  9.69 us (1%)
    reduce_scatter x1, waiting for transfers between devices, body(): lax.psum_scatter(column_part, 'node', scatter_dimension=0, tiled=True)  199 us
    all_to_all x1, waiting for transfers between devices, body(): compact = jnp.concatenate(lax.all_to_all(repeated, 'node', 0, 0), axis=0)  123 us
    scatter-add x1, other arithmetic, body(): jnp.zeros((compact_cols, block, feat), jnp.float32).at[slot_cols]  91.2 us
    scatter-add x1, other arithmetic, body(): partial_agg = jnp.zeros((row_blocks, block, feat), jnp.float32).at[slot_r...  56.7 us
    psum x1, blocking collectives, body(): aggregated = lax.psum(partial_agg, 'rep').astype(jnp.bfloat16)  42.7 us
    mul x1, local copies, waits for them, and re-layouts, body(): jnp.einsum('tab,taf->tbf', slot_tiles, dagg_blocks[slot_rows], preferred_...  41.7 us
    mul x1, local copies, waits for them, and re-layouts, body(): jnp.einsum('tab,tbf->taf', slot_tiles, picked, preferred_element_type=jnp...  41.6 us
    dot_general x1, matrix products, body(): jnp.einsum('tab,tbf->taf', slot_tiles, picked, preferred_element_type=jnp...  30.3 us
  transfers between devices with their start and end apart: 4, of which 2 were waited for; matrix products, arithmetic and copies ran while one was open for 44% of the time, Pallas kernels for 0%

profile of v1, /device:TPU:0, one launch (start us, length us, event | category | flops | bytes accessed | tf_op | source)
XLA Modules:
  0.0 725.4 jit_solution(5454022224339401305)
XLA Ops:
  7.2 0.0 copy-start
  7.2 1.2 copy-done
  8.4 4.2 stack.2
  12.7 9.4 %all-to-all-start = ((bf16[32,2,256,256]{3,2,1,0:T(8,128)(2,1)}), bf16[32,2,256,256]{3,2,1,0:T(8,128)(2,1)}, u32[]{:S(2)}, u32[]{:S(2)}) async-start(bf16[32,2,256,256]{3,2,1,0:T(8,128)(2,1)} %stack.2), calls=%async_computation | async-start | bytes 16777216 | tf_op jit(solution)/shard_map/all_to_all | solution.py:26
  22.1 0.0 all-gather.2.cloned.1.call-start
  22.1 0.7 all-gather.2.cloned.1.call-update
  22.8 0.0 all-reduce.3.cloned.1.call-start
  23.5 0.0 copy-start.4
  23.6 123.0 %all-to-all-done = bf16[32,2,256,256]{3,2,1,0:T(8,128)(2,1)} async-done(((bf16[32,2,256,256]{3,2,1,0:T(8,128)(2,1)}), bf16[32,2,256,256]{3,2,1,0:T(8,128)(2,1)}, u32[]{:S(2)}, u32[]{:S(2)}) %all-to-all-start) | async-done | bytes 8388640 | tf_op jit(solution)/shard_map/all_to_all | solution.py:26
  146.6 13.0 %gather_fusion = bf16[160,256,256]{2,1,0:T(8,128)(2,1)} fusion(bf16[64,256,256]{2,1,0:T(8,128)(2,1)} %bitcast.3, s32[1024]{0:T(1024)S(1)} %pad_clamp_fusion.1), kind=kCustom, calls=%fused_computation | custom fusion | bytes 41943680 | tf_op jit(solution)/shard_map/gather | solution.py:27
  159.6 30.3 %multiply_bitcast_fusion.1 = f32[160,256,256]{1,2,0:T(8,128)} fusion(f32[160]{0:T(256)S(1)} %compare_convert_fusion, bf16[160,256,256]{2,1,0:T(8,128)(2,1)} %gather_fusion, bf16[1,1,160,256,256]{4,3,2,1,0:T(8,128)(2,1)} %param.10), kind=kOutput, calls=%fused_computation.5 | convolution fusion | flops 5379194880 | bytes 83886720 | tf_op jit(solution)/shard_map/tab,tbf->taf/dot_general | solution.py:29
  189.9 41.6 %copy.13 = f32[160,256,256]{2,1,0:T(8,128)} copy(f32[160,256,256]{1,2,0:T(8,128)} %multiply_bitcast_fusion.1) | data formatting | bytes 83886080 | tf_op jit(solution)/shard_map/mul | solution.py:29
  231.5 0.2 broadcast_in_dim.4
  231.7 0.0 copy-start.3
  231.7 56.7 %scatter_fusion = f32[8,256,256]{2,1,0:T(8,128)S(1)} fusion(f32[8,256,256]{2,1,0:T(8,128)S(1)} %broadcast_in_dim.4, s32[160]{0:T(256)S(1)} %bitcast.39, f32[160,256,256]{2,1,0:T(8,128)} %copy.13), kind=kCustom, calls=%fused_computation.2 | custom fusion | flops 10485760 | bytes 125829760 | tf_op jit(solution)/shard_map/scatter-add | solution.py:35
  288.4 42.7 %all-reduce.4 = bf16[2048,256]{1,0:T(8,128)(2,1)S(1)} all-reduce(f32[2048,256]{1,0:T(8,128)S(1)} %bitcast.33), channel_id=1, replica_groups=mesh['node'=32,'rep'=4] {'rep'}, use_global_device_ids=true, to_apply=%region_1.0 | all-reduce | flops 524288 | bytes 3145728 | tf_op jit(solution)/shard_map/psum | solution.py:39
  331.1 0.0 all-gather.2.cloned.1.call-done
  331.1 3.8 multiply_convert_fusion
  334.9 0.5 convolution_convert_fusion
  335.4 1.9 fusion.9
  337.3 0.0 all-reduce.3.cloned.1.call-update
  337.3 0.2 reduce-scatter.2.cloned.1.call-start
  337.5 9.6 %gather_fusion.1 = bf16[160,256,256]{2,1,0:T(8,128)(2,1)} fusion(bf16[8,256,256]{2,1,0:T(8,128)(2,1)S(1)} %bitcast.34, s32[1024]{0:T(1024)S(1)} %pad_clamp_fusion), kind=kCustom, calls=%fused_computation.1 | custom fusion | bytes 41943680 | tf_op jit(solution)/shard_map/gather | solution.py:56
  347.1 26.6 %multiply_bitcast_fusion = f32[160,256,256]{1,2,0:T(8,128)} fusion(f32[160]{0:T(256)S(1)} %compare_convert_fusion, bf16[160,256,256]{2,1,0:T(8,128)(2,1)} %gather_fusion.1, bf16[1,1,160,256,256]{4,3,2,1,0:T(8,128)(2,1)} %param.10), kind=kOutput, calls=%fused_computation.4 | convolution fusion | flops 5379194880 | bytes 83886720 | tf_op jit(solution)/shard_map/tab,taf->tbf/dot_general | solution.py:55
  373.7 41.7 %copy.15 = f32[160,256,256]{2,1,0:T(8,128)} copy(f32[160,256,256]{1,2,0:T(8,128)} %multiply_bitcast_fusion) | data formatting | bytes 83886080 | tf_op jit(solution)/shard_map/mul | solution.py:55
  415.4 7.8 %broadcast_in_dim.5 = f32[64,256,256]{2,1,0:T(8,128)} broadcast(f32[]{:T(128)} %constant.10.clone.1), dimensions={} | broadcast | bytes 16777220 | tf_op jit(solution)/shard_map/broadcast_in_dim | solution.py:61
  423.2 91.2 %scatter_fusion.1 = f32[64,256,256]{2,1,0:T(8,128)} fusion(f32[64,256,256]{2,1,0:T(8,128)} %broadcast_in_dim.5, s32[160]{0:T(256)S(1)} %bitcast.37, f32[160,256,256]{2,1,0:T(8,128)} %copy.15), kind=kCustom, calls=%fused_computation.3 | custom fusion | flops 10485760 | bytes 125829760 | tf_op jit(solution)/shard_map/scatter-add | solution.py:61
  514.4 0.0 reduce-scatter.2.cloned.1.call-update
  514.4 1.8 fusion.8
  516.2 1.7 broadcast_multiply_fusion
  517.9 199.1 %reduce-scatter.2.cloned.1.call-done = f32[2,256,256]{2,1,0:T(8,128)} async-done(((f32[64,256,256]{2,1,0:T(8,128)}), f32[2,256,256]{2,1,0:T(8,128)}) %reduce-scatter.2.cloned.1.call-update) | async-done | bytes 524304 | tf_op jit(solution)/shard_map/reduce_scatter | solution.py:63
  717.0 1.8 convert_element_type.34
  (18 shorter events, 0.1 us)
Async XLA Ops:
  7.2 1.2 copy-start
  7.2 16.3 %copy-start.7 = (s32[1,1,160]{2,1,0:T(1,128)S(1)}, s32[1,1,160]{2,1,0:T(1,128)}, u32[]{:S(2)}) copy-start(s32[1,1,160]{2,1,0:T(1,128)} %param.11) | copy-start | bytes 1924
  7.2 16.3 %copy-start.6 = (s32[1,1,160]{2,1,0:T(1,128)S(1)}, s32[1,1,160]{2,1,0:T(1,128)}, u32[]{:S(2)}) copy-start(s32[1,1,160]{2,1,0:T(1,128)} %param.12) | copy-start | bytes 1924
  12.7 133.9 %all-to-all-start = ((bf16[32,2,256,256]{3,2,1,0:T(8,128)(2,1)}), bf16[32,2,256,256]{3,2,1,0:T(8,128)(2,1)}, u32[]{:S(2)}, u32[]{:S(2)}) async-start(bf16[32,2,256,256]{3,2,1,0:T(8,128)(2,1)} %stack.2), calls=%async_computation | async-start | bytes 16777216 | tf_op jit(solution)/shard_map/all_to_all | solution.py:26
  22.1 309.0 %all-gather.2.cloned.1.call-start = ((), (), s32[]{:S(2)}) async-start(), calls=%async_computation.2 | async-start | bytes 1310720 | tf_op jit(solution)/shard_map/all_gather | solution.py:40
  22.8 493.4 %all-reduce.3.cloned.1.call-start = ((), (), s32[]{:S(2)}) async-start(), calls=%async_computation.4 | async-start | bytes 524288 | tf_op jit(solution)/shard_map/psum | solution.py:52
  23.5 136.1 %copy-start.4 = (s32[160,1]{0,1:T(1,128)}, s32[160,1]{0,1:T(1,128)S(1)}, u32[]{:S(2)}) copy-start(s32[160,1]{0,1:T(1,128)S(1)} %get-tuple-element.6) | copy-start | bytes 1924
  231.7 99.4 %copy-start.3 = (bf16[256,256]{1,0:T(8,128)(2,1)S(1)}, bf16[256,256]{1,0:T(8,128)(2,1)}, u32[]{:S(2)}) copy-start(bf16[256,256]{1,0:T(8,128)(2,1)} %param.8) | copy-start | bytes 393220
  331.1 3.8 copy-start.2
  337.3 379.7 %reduce-scatter.2.cloned.1.call-start = ((), (), s32[]{:S(2)}) async-start(), calls=%async_computation.3 | async-start | bytes 17301504 | tf_op jit(solution)/shard_map/reduce_scatter | solution.py:63
  373.7 49.5 %copy-start.5 = (s32[160,1]{0,1:T(1,128)S(1)}, s32[160,1]{0,1:T(1,128)}, u32[]{:S(2)}) copy-start(s32[160,1]{0,1:T(1,128)} %copy-done.4) | copy-start | bytes 1924
  423.2 295.6 %copy-start.1 = (bf16[2048,256]{1,0:T(8,128)(2,1)S(1)}, bf16[2048,256]{1,0:T(8,128)(2,1)}, u32[]{:S(2)}) copy-start(bf16[2048,256]{1,0:T(8,128)(2,1)} %param.7) | copy-start | bytes 3145732
Sparse Core Ops, SparseCore 0:
  24.6 58.2 all-gather.1
  337.4 140.1 all-reduce.2
  514.5 202.4 reduce-scatter.1
